TPU v7x, 32 devices: a whole 2x2x4 slice. The times are simulated.
32 devices in a mesh: parts: 2 (over x), dp: 4 (over y, core), shard: 4 (over z).
Axes of the slice: x: 2, y: 2, z: 4, core: 2. Of those that a mesh axis runs over, the one named last changes fastest.
Arguments:
- projected: bfloat16 [7680, 7680], P(('parts', 'dp', 'shard')), parts along dimension 0, may hold values from -4 to 4
- residual: bfloat16 [7680, 2560], P(('parts', 'dp', 'shard')), parts along dimension 0, may hold values from -6 to 6
- out_weight: bfloat16 [2560, 2560], P(None, 'shard'), may hold values from -0.125 to 0.125
- probe_weight: bfloat16 [2, 2560, 8], replicated, may hold values from -0.125 to 0.125
- labels: int32 [7680], P(('parts', 'dp', 'shard')), parts along dimension 0, may hold values from 0 to 7
- lengths: int32 [32, 9], P(('parts', 'dp', 'shard')), parts along dimension 0, may hold values from 12 to 48, as said below
- destination: int32 [32, 9], P(('parts', 'dp', 'shard')), parts along dimension 0, may hold values from 0 to 3, as said below
Outputs:
- hidden_rows: bfloat16 [18432, 2560], P(('parts', 'dp', 'shard')), parts along dimension 0
- probe_grad: float32 [4, 2560, 8], P('parts'), parts along dimension 0
There are 2 independent parts, one for each index of `parts`. A program takes and returns all parts, laid end to end along the dimension named above; an argument that names none is the same for every part. Nothing has to cross between parts.
Inputs may be any that keep to these rules, and one draw needn't show every extreme that they name: Each row of lengths sums to 240 and holds exactly one protein of length 48. `destination`: A loader assigns at most 3 proteins to any one dp index; in every shard column one dp index is assigned exactly 3 proteins by every loader of that column.
All inputs are finite; a program needn't handle non-finite values.
Results may differ from a plain program's by a relative error of at most 0.0031.
Values may be sent and summed in bfloat16 or wider, within the bound.
No kernel may reach another device: no remote copies, remote signals or barrier semaphores. Data moves between devices by JAX's collectives and lax.ppermute only.
A program may use at most 128 MiB of HBM per device.

v0:
```python
import jax
import jax.numpy as jnp
from jax import lax
from jax.sharding import PartitionSpec as P

HS = 128
CLASSES = 8
LMAX = 48
TOK_DEV = 240


def attend(blocks, block_lengths):
    block_count = blocks.shape[0]
    span_rows = blocks.shape[1]
    head_width = blocks.shape[2] // 3
    head_count = head_width // HS
    queries = blocks[:, :, :head_width].reshape(block_count, span_rows, head_count, HS)
    key_rows = blocks[:, :, head_width : 2 * head_width].reshape(
        block_count, span_rows, head_count, HS
    )
    value_rows = blocks[:, :, 2 * head_width :].reshape(block_count, span_rows, head_count, HS)
    scores = jnp.einsum(
        "plhs,pmhs->phlm", queries, key_rows, preferred_element_type=jnp.float32
    ) * HS ** (-0.5)
    keep_mask = (jnp.arange(span_rows, dtype=jnp.int32)[None, :] < block_lengths[:, None]).astype(
        jnp.float32
    )
    weights = jnp.exp(scores) * keep_mask[:, None, None, :]
    denominator = (
        jnp.sum(weights, axis=-1, keepdims=True)
        + (block_lengths == 0).astype(jnp.float32)[:, None, None, None]
    )
    weight_low = (weights / denominator).astype(jnp.bfloat16)
    attended = jnp.einsum(
        "phlm,pmhs->plhs", weight_low, value_rows, preferred_element_type=jnp.float32
    )
    return attended.reshape(block_count * span_rows, head_width).astype(jnp.bfloat16)


def project(attended, out_weight):
    return jnp.dot(
        attended,
        lax.all_gather(out_weight, "shard", axis=1, tiled=True),
        preferred_element_type=jnp.float32,
    )


def probe_terms(represent_x, represent_h, label_rows, keep_mask, probe_weight):
    one_hot = (label_rows[:, None] == jnp.arange(CLASSES, dtype=jnp.int32)[None, :]).astype(
        jnp.float32
    )
    collected = []
    for which, represent in enumerate((represent_x, represent_h)):
        logits = jnp.dot(represent, probe_weight[which], preferred_element_type=jnp.float32)
        exponent = jnp.exp(logits)
        likelihood = exponent / jnp.sum(exponent, axis=1, keepdims=True)
        mismatch = ((likelihood - one_hot) * keep_mask[:, None] / TOK_DEV).astype(jnp.bfloat16)
        collected.append(
            lax.dot_general(
                represent, mismatch, (((0,), (0,)), ((), ())), preferred_element_type=jnp.float32
            )
        )
    return jnp.stack(collected)


def per_device(projected, residual, out_weight, probe_weight, labels, lengths, destination):
    group_size = lax.axis_size("dp")
    prot_count = lengths.shape[1]
    slot_count = -(-prot_count // group_size)
    tok_count = projected.shape[0]
    lens_own = lengths[0]
    dest_own = destination[0]
    starts = jnp.cumsum(lens_own) - lens_own
    offsets = jnp.arange(LMAX, dtype=jnp.int32)
    positions = jnp.arange(prot_count, dtype=jnp.int32)
    same_dest = dest_own[:, None] == dest_own[None, :]
    earlier = positions[:, None] > positions[None, :]
    slot_rank = jnp.sum((same_dest & earlier).astype(jnp.int32), axis=1)
    slot_match = (
        dest_own[None, None, :] == jnp.arange(group_size, dtype=jnp.int32)[:, None, None]
    ) & (slot_rank[None, None, :] == jnp.arange(slot_count, dtype=jnp.int32)[None, :, None])
    match_int = slot_match.astype(jnp.int32)
    slot_start = jnp.sum(match_int * starts, axis=2)
    slot_len = jnp.sum(match_int * lens_own, axis=2)
    block_count = group_size * slot_count
    row_index = jnp.minimum(slot_start[:, :, None] + offsets, tok_count - 1).reshape(
        group_size, slot_count * LMAX
    )
    live_rows = (offsets[None, None, :] < slot_len[:, :, None]).reshape(
        group_size, slot_count * LMAX
    )
    rows_send = jnp.where(live_rows[:, :, None], jnp.take(projected, row_index, axis=0), 0)
    resid_send = jnp.where(live_rows[:, :, None], jnp.take(residual, row_index, axis=0), 0)
    label_send = jnp.where(live_rows, jnp.take(labels, row_index), 0)
    got_labels, got_lengths = (
        lax.all_to_all(label_send, "dp", split_axis=0, concat_axis=0, tiled=True),
        lax.all_to_all(slot_len, "dp", split_axis=0, concat_axis=0, tiled=True),
    )
    got_rows, got_resid = (
        lax.all_to_all(rows_send, "dp", split_axis=0, concat_axis=0, tiled=True),
        lax.all_to_all(resid_send, "dp", split_axis=0, concat_axis=0, tiled=True),
    )
    lengths_recv = got_lengths.reshape(block_count)
    attended = attend(got_rows.reshape(block_count, LMAX, -1), lengths_recv)
    keep_mask = (offsets[None, :] < lengths_recv[:, None]).astype(jnp.float32).reshape(-1)
    represent = got_resid.reshape(block_count * LMAX, -1)
    mixed_rows = project(attended, out_weight) + represent.astype(jnp.float32)
    hidden = (mixed_rows * keep_mask[:, None]).astype(jnp.bfloat16)
    grad_terms = probe_terms(represent, hidden, got_labels.reshape(-1), keep_mask, probe_weight)
    grad_sum = lax.psum(grad_terms, ("dp", "shard"))
    return (hidden, grad_sum)


def solution(mesh):
    return jax.shard_map(
        per_device,
        mesh=mesh,
        in_specs=(
            P(("parts", "dp", "shard"), None),
            P(("parts", "dp", "shard"), None),
            P(None, "shard"),
            P(),
            P(("parts", "dp", "shard")),
            P(("parts", "dp", "shard"), None),
            P(("parts", "dp", "shard"), None),
        ),
        out_specs=(P(("parts", "dp", "shard"), None), P("parts", None, None)),
        check_vma=False,
    )
```

profile of v0, /device:TPU:8, one launch (start us, length us, event | category | flops | bytes accessed | tf_op | source)
XLA Modules:
  0.0 349.7 jit_solution(5877579920904036037)
XLA Ops:
  7.2 0.7 all-gather.2.cloned.1.call-update
  8.3 0.2 fusion.37
  8.5 0.7 copy.27
  9.2 3.2 all-to-all-start.1
  13.4 4.2 %gather_fusion.1 = bf16[576,2560]{1,0:T(8,128)(2,1)} fusion(bf16[240,2560]{1,0:T(8,128)(2,1)S(1)} %copy-done, s32[1024]{0:T(1024)S(1)} %pad_clamp_fusion), kind=kCustom, calls=%fused_computation.1 | custom fusion | bytes 5900544 | tf_op jit(solution)/shard_map/jit(_take)/gather | solution.py:93
  17.6 3.9 %gather_fusion.2 = s32[576]{0:T(1024)S(1)} fusion(s32[240]{0:T(256)S(1)} %copy-done.2, s32[1024]{0:T(1024)S(1)} %pad_clamp_fusion), kind=kCustom, calls=%fused_computation.2 | custom fusion | bytes 6912 | tf_op jit(solution)/shard_map/jit(_take)/gather | solution.py:94
  21.6 0.6 copy.31
  22.3 3.3 all-to-all-start.3
  25.5 4.2 %select_select_fusion.1 = bf16[4,144,2560]{2,1,0:T(8,128)(2,1)} fusion(bf16[4,144,2560]{2,1,0:T(8,128)(2,1)} %bitcast.61, pred[4,144]{1,0:T(4,128)(4,1)S(1)} %get-tuple-element.8, pred[4,144]{1,0:T(4,128)(4,1)S(1)} %get-tuple-element.7), kind=kLoop, calls=%fused_computation.23 | loop fusion | flops 2949120 | bytes 5899392 | tf_op jit(solution)/shard_map/jit(_where)/select_n | solution.py:93
  29.7 22.4 %gather_fusion = bf16[576,7680]{1,0:T(8,128)(2,1)} fusion(bf16[240,7680]{1,0:T(8,128)(2,1)} %param.7, s32[1024]{0:T(1024)S(1)} %pad_clamp_fusion), kind=kCustom, calls=%fused_computation | custom fusion | bytes 17697024 | tf_op jit(solution)/shard_map/jit(_take)/gather | solution.py:92
  52.1 4.6 %all-to-all-start.2 = ((bf16[4,144,2560]{2,1,0:T(8,128)(2,1)}), bf16[4,144,2560]{2,1,0:T(8,128)(2,1)}, u32[]{:S(2)}, u32[]{:S(2)}) async-start(bf16[4,144,2560]{2,1,0:T(8,128)(2,1)} %select_select_fusion.1), calls=%async_computation.2 | async-start | bytes 5898240 | tf_op jit(solution)/shard_map/all_to_all | solution.py:101
  56.8 8.1 %select_select_fusion = bf16[4,144,7680]{2,1,0:T(8,128)(2,1)} fusion(bf16[4,144,7680]{2,1,0:T(8,128)(2,1)} %bitcast.60, pred[4,144]{1,0:T(4,128)(4,1)S(1)} %get-tuple-element.8, pred[4,144]{1,0:T(4,128)(4,1)S(1)} %get-tuple-element.7), kind=kLoop, calls=%fused_computation.3 | loop fusion | flops 8847360 | bytes 17695872 | tf_op jit(solution)/shard_map/jit(_where)/select_n | solution.py:92
  64.9 26.7 %all-to-all-done.2 = bf16[4,144,2560]{2,1,0:T(8,128)(2,1)} async-done(((bf16[4,144,2560]{2,1,0:T(8,128)(2,1)}), bf16[4,144,2560]{2,1,0:T(8,128)(2,1)}, u32[]{:S(2)}, u32[]{:S(2)}) %all-to-all-start.2) | async-done | bytes 2949152 | tf_op jit(solution)/shard_map/all_to_all | solution.py:101
  91.6 5.7 %all-to-all-start = ((bf16[4,144,7680]{2,1,0:T(8,128)(2,1)}), bf16[4,144,7680]{2,1,0:T(8,128)(2,1)}, u32[]{:S(2)}, u32[]{:S(2)}) async-start(bf16[4,144,7680]{2,1,0:T(8,128)(2,1)} %select_select_fusion), calls=%async_computation | async-start | bytes 17694720 | tf_op jit(solution)/shard_map/all_to_all | solution.py:100
  97.3 0.2 all-reduce.2.cloned.1.call-start
  97.6 0.5 broadcast.237
  98.1 0.7 reduce.4
  99.1 2.7 fusion.43
  101.8 2.3 convolution_bitcast_fusion.1
  104.1 91.3 %all-to-all-done = bf16[4,144,7680]{2,1,0:T(8,128)(2,1)} async-done(((bf16[4,144,7680]{2,1,0:T(8,128)(2,1)}), bf16[4,144,7680]{2,1,0:T(8,128)(2,1)}, u32[]{:S(2)}, u32[]{:S(2)}) %all-to-all-start) | async-done | bytes 8847392 | tf_op jit(solution)/shard_map/all_to_all | solution.py:100
  195.4 4.0 %slice_bitcast_fusion.2 = (bf16[12,6,20,8,128]{4,3,2,1,0:T(8,128)(2,1)S(1)}, bf16[12,6,20,8,128]{4,3,2,1,0:T(8,128)(2,1)S(1)}, bf16[12,6,20,8,128]{4,3,2,1,0:T(8,128)(2,1)S(1)}) fusion(bf16[12,48,7680]{2,1,0:T(8,128)(2,1)} %bitcast.5), kind=kLoop, calls=%fused_computation.22 | loop fusion | bytes 17694720
  199.4 1.7 fusion
  201.2 2.0 convert_bitcast_fusion
  203.2 2.6 copy.30
  205.8 28.8 %all-gather.2.cloned.1.call-done = bf16[2560,2560]{1,0:T(8,128)(2,1)} async-done(((bf16[2560,640]{1,0:T(8,128)(2,1)}), bf16[2560,2560]{1,0:T(8,128)(2,1)}) %all-gather.2.cloned.1.call-update) | async-done | bytes 13107216 | tf_op jit(solution)/shard_map/all_gather | solution.py:43
  234.6 12.4 %multiply_convert_fusion = bf16[576,2560]{1,0:T(8,128)(2,1)S(1)} fusion(bf16[576,2560]{1,0:T(8,128)(2,1)} %bitcast.9, bf16[2560,2560]{1,0:T(8,128)(2,1)} %all-gather.2.cloned.1.call-done, bf16[72,8,20,128]{3,2,1,0:T(8,128)(2,1)} %bitcast.62, f32[576]{0:T(1024)S(1)} %reshape.360), kind=kOutput, calls=%fused_computation.4 | convolution fusion | flops 7555645440 | bytes 21956864 | tf_op jit(solution)/shard_map/dot_general | solution.py:41
  246.9 0.9 fusion.42
  247.8 0.5 convolution_bitcast_fusion
  248.3 0.2 copy-done.3
  248.5 0.7 pad_maximum_fusion
  249.2 92.0 %all-reduce.2.cloned.1.call-done = f32[2,2560,8]{1,2,0:T(8,128)} async-done(((f32[2,2560,8]{1,2,0:T(8,128)}), f32[2,2560,8]{1,2,0:T(8,128)}) %all-reduce.2.cloned.1.call-update) | async-done | bytes 163856 | tf_op jit(solution)/shard_map/psum | solution.py:110
  341.3 1.6 copy.62
  (46 shorter events, 1.9 us)
Async XLA Ops:
  7.2 6.2 %copy-start = (bf16[240,2560]{1,0:T(8,128)(2,1)S(1)}, bf16[240,2560]{1,0:T(8,128)(2,1)}, u32[]{:S(2)}) copy-start(bf16[240,2560]{1,0:T(8,128)(2,1)} %param.8) | copy-start | bytes 3686404
  7.2 0.8 copy-start.5
  7.2 0.9 copy-start.6
  7.2 227.4 %all-gather.2.cloned.1.call-start = ((), (), s32[]{:S(2)}) async-start(), calls=%async_computation.4 | async-start | bytes 16384000 | tf_op jit(solution)/shard_map/all_gather | solution.py:43
  9.2 13.1 %all-to-all-start.1 = ((s32[4,1,3]{2,1,0:T(1,128)}), s32[4,1,3]{2,1,0:T(1,128)S(1)}, u32[]{:S(2)}, u32[]{:S(2)}) async-start(s32[4,1,3]{2,1,0:T(1,128)} %copy.27), calls=%async_computation.1 | async-start | bytes 4096 | tf_op jit(solution)/shard_map/all_to_all | solution.py:97
  13.4 4.2 %copy-start.2 = (s32[240]{0:T(256)S(1)}, s32[240]{0:T(256)}, u32[]{:S(2)}) copy-start(s32[240]{0:T(256)} %param.11) | copy-start | bytes 2884
  22.3 29.9 %all-to-all-start.3 = ((s32[4,1,144]{2,1,0:T(1,128)}), s32[4,1,144]{2,1,0:T(1,128)S(1)}, u32[]{:S(2)}, u32[]{:S(2)}) async-start(s32[4,1,144]{2,1,0:T(1,128)} %copy.31), calls=%async_computation.3 | async-start | bytes 8192 | tf_op jit(solution)/shard_map/all_to_all | solution.py:96
  52.1 39.5 %all-to-all-start.2 = ((bf16[4,144,2560]{2,1,0:T(8,128)(2,1)}), bf16[4,144,2560]{2,1,0:T(8,128)(2,1)}, u32[]{:S(2)}, u32[]{:S(2)}) async-start(bf16[4,144,2560]{2,1,0:T(8,128)(2,1)} %select_select_fusion.1), calls=%async_computation.2 | async-start | bytes 5898240 | tf_op jit(solution)/shard_map/all_to_all | solution.py:101
  64.9 34.2 %copy-start.4 = (bf16[2,2560,8]{1,2,0:T(8,128)(2,1)S(1)}, bf16[2,2560,8]{1,2,0:T(8,128)(2,1)}, u32[]{:S(2)}) copy-start(bf16[2,2560,8]{1,2,0:T(8,128)(2,1)} %param.10) | copy-start | bytes 245764
  91.6 103.8 %all-to-all-start = ((bf16[4,144,7680]{2,1,0:T(8,128)(2,1)}), bf16[4,144,7680]{2,1,0:T(8,128)(2,1)}, u32[]{:S(2)}, u32[]{:S(2)}) async-start(bf16[4,144,7680]{2,1,0:T(8,128)(2,1)} %select_select_fusion), calls=%async_computation | async-start | bytes 17694720 | tf_op jit(solution)/shard_map/all_to_all | solution.py:100
  97.3 244.0 %all-reduce.2.cloned.1.call-start = ((), (), s32[]{:S(2)}) async-start(), calls=%async_computation.5 | async-start | bytes 327680 | tf_op jit(solution)/shard_map/psum | solution.py:110
  246.9 1.6 copy-start.3
  247.8 95.0 %copy-start.1 = (bf16[240,2560]{1,0:T(8,128)(2,1)S(1)}, bf16[240,2560]{1,0:T(8,128)(2,1)}, u32[]{:S(2)}) copy-start(bf16[240,2560]{1,0:T(8,128)(2,1)} %param.8) | copy-start | bytes 3686404
Sparse Core Ops, SparseCore 0:
  9.6 224.9 all-gather.1
  249.4 91.8 all-reduce.1
where the time goes:
time: 350 us
  waiting for transfers between devices  239 us (68%)
  local copies, waits for them, and re-layouts  42 us (12%)
  matrix products  22.5 us (6%)
  starting transfers between devices  17 us (5%)
  other arithmetic  14.4 us (4%)
  between operations  14.3 us (4%)
    psum x1, waiting for transfers between devices, per_device(): grad_sum = lax.psum(grad_terms, ('dp', 'shard'))  92 us
    all_to_all x1, waiting for transfers between devices, per_device(): lax.all_to_all(rows_send, 'dp', split_axis=0, concat_axis=0, tiled=True)  91.3 us
    all_gather x1, waiting for transfers between devices, project(): lax.all_gather(out_weight, 'shard', axis=1, tiled=True)  28.8 us
    all_to_all x1, waiting for transfers between devices, per_device(): lax.all_to_all(resid_send, 'dp', split_axis=0, concat_axis=0, tiled=True)  26.7 us
    gather x1, local copies, waits for them, and re-layouts, per_device(): jnp.take(projected, row_index, axis=0)  22.4 us
    dot_general x1, matrix products, project(): jnp.dot(attended, lax.all_gather(out_weight, 'shard', axis=1, tiled=True)...  12.4 us
    select_n x1, other arithmetic, per_device(): jnp.where(live_rows[:, :, None], jnp.take(projected, row_index, axis=0), 0)  8.14 us
  transfers between devices with their start and end apart: 6, of which 4 were waited for; matrix products, arithmetic and copies ran while one was open for 18% of the time, Pallas kernels for 0%

commit v1 on v0

--- a/solution.py
+++ b/solution.py
@@ -107,7 +107,8 @@
     mixed_rows = project(attended, out_weight) + represent.astype(jnp.float32)
     hidden = (mixed_rows * keep_mask[:, None]).astype(jnp.bfloat16)
     grad_terms = probe_terms(represent, hidden, got_labels.reshape(-1), keep_mask, probe_weight)
-    grad_sum = lax.psum(grad_terms, ("dp", "shard"))
+    terms = lax.all_gather(grad_terms, ("dp", "shard"))
+    grad_sum = jnp.sum(terms, axis=0)
     return (hidden, grad_sum)
 
 

time: 350 us -> 305 us (0.87)
  waiting for transfers between devices: 239 us -> 192 us
    psum x1 -> x0, waiting for transfers between devices: 92 us -> none  [per_device(): grad_sum = lax.psum(grad_terms, ('dp', 'shard'))]
    all_gather x0 -> x1, waiting for transfers between devices: none -> 44.1 us  [per_device(): terms = lax.all_gather(grad_terms, ('dp', 'shard'))]
  transfers between devices with their start and end apart: 6 -> 6, of which waited for: 4 -> 4; matrix products, arithmetic and copies ran while one was open for 18% -> 21% of each run, Pallas kernels for 0% -> 0%
where the time goes in v1:
time: 305 us; the launch traced here: 303 us
  waiting for transfers between devices  192 us (63%)
  local copies, waits for them, and re-layouts  40.4 us (13%)
  matrix products  22.5 us (7%)
  starting transfers between devices  17 us (6%)
  other arithmetic  17 us (6%)
  between operations  14.3 us (5%)
    all_to_all x1, waiting for transfers between devices, per_device(): lax.all_to_all(rows_send, 'dp', split_axis=0, concat_axis=0, tiled=True)  91.3 us
    all_gather x1, waiting for transfers between devices, per_device(): terms = lax.all_gather(grad_terms, ('dp', 'shard'))  44.1 us
    all_gather x1, waiting for transfers between devices, project(): lax.all_gather(out_weight, 'shard', axis=1, tiled=True)  28.8 us
    all_to_all x1, waiting for transfers between devices, per_device(): lax.all_to_all(resid_send, 'dp', split_axis=0, concat_axis=0, tiled=True)  26.7 us
    gather x1, local copies, waits for them, and re-layouts, per_device(): jnp.take(projected, row_index, axis=0)  22.4 us
    dot_general x1, matrix products, project(): jnp.dot(attended, lax.all_gather(out_weight, 'shard', axis=1, tiled=True)...  12.4 us
    select_n x1, other arithmetic, per_device(): jnp.where(live_rows[:, :, None], jnp.take(projected, row_index, axis=0), 0)  8.14 us
  transfers between devices with their start and end apart: 6, of which 4 were waited for; matrix products, arithmetic and copies ran while one was open for 21% of the time, Pallas kernels for 0%

profile of v1, /device:TPU:8, one launch (start us, length us, event | category | flops | bytes accessed | tf_op | source)
XLA Modules:
  0.0 302.7 jit_solution(11174682310982965623)
XLA Ops:
  7.2 0.7 all-gather.4.cloned.1.call-update
  8.3 0.2 fusion.37
  8.5 0.7 copy.27
  9.2 3.2 %all-to-all-start.1 = ((s32[4,1,3]{2,1,0:T(1,128)}), s32[4,1,3]{2,1,0:T(1,128)S(1)}, u32[]{:S(2)}, u32[]{:S(2)}) async-start(s32[4,1,3]{2,1,0:T(1,128)} %copy.27), calls=%async_computation.1 | async-start | bytes 4096 | tf_op jit(solution)/shard_map/all_to_all | solution.py:97
  13.4 4.2 %gather_fusion.1 = bf16[576,2560]{1,0:T(8,128)(2,1)} fusion(bf16[240,2560]{1,0:T(8,128)(2,1)S(1)} %copy-done, s32[1024]{0:T(1024)S(1)} %pad_clamp_fusion), kind=kCustom, calls=%fused_computation.1 | custom fusion | bytes 5900544 | tf_op jit(solution)/shard_map/jit(_take)/gather | solution.py:93
  17.6 3.9 %gather_fusion.2 = s32[576]{0:T(1024)S(1)} fusion(s32[240]{0:T(256)S(1)} %copy-done.2, s32[1024]{0:T(1024)S(1)} %pad_clamp_fusion), kind=kCustom, calls=%fused_computation.2 | custom fusion | bytes 6912 | tf_op jit(solution)/shard_map/jit(_take)/gather | solution.py:94
  21.6 0.6 copy.31
  22.3 3.3 %all-to-all-start.3 = ((s32[4,1,144]{2,1,0:T(1,128)}), s32[4,1,144]{2,1,0:T(1,128)S(1)}, u32[]{:S(2)}, u32[]{:S(2)}) async-start(s32[4,1,144]{2,1,0:T(1,128)} %copy.31), calls=%async_computation.3 | async-start | bytes 8192 | tf_op jit(solution)/shard_map/all_to_all | solution.py:96
  25.5 4.2 %select_select_fusion.1 = bf16[4,144,2560]{2,1,0:T(8,128)(2,1)} fusion(bf16[4,144,2560]{2,1,0:T(8,128)(2,1)} %bitcast.62, pred[4,144]{1,0:T(4,128)(4,1)S(1)} %get-tuple-element.8, pred[4,144]{1,0:T(4,128)(4,1)S(1)} %get-tuple-element.7), kind=kLoop, calls=%fused_computation.23 | loop fusion | flops 2949120 | bytes 5899392 | tf_op jit(solution)/shard_map/jit(_where)/select_n | solution.py:93
  29.7 22.4 %gather_fusion = bf16[576,7680]{1,0:T(8,128)(2,1)} fusion(bf16[240,7680]{1,0:T(8,128)(2,1)} %param.7, s32[1024]{0:T(1024)S(1)} %pad_clamp_fusion), kind=kCustom, calls=%fused_computation | custom fusion | bytes 17697024 | tf_op jit(solution)/shard_map/jit(_take)/gather | solution.py:92
  52.1 4.6 %all-to-all-start.2 = ((bf16[4,144,2560]{2,1,0:T(8,128)(2,1)}), bf16[4,144,2560]{2,1,0:T(8,128)(2,1)}, u32[]{:S(2)}, u32[]{:S(2)}) async-start(bf16[4,144,2560]{2,1,0:T(8,128)(2,1)} %select_select_fusion.1), calls=%async_computation.2 | async-start | bytes 5898240 | tf_op jit(solution)/shard_map/all_to_all | solution.py:101
  56.8 8.1 %select_select_fusion = bf16[4,144,7680]{2,1,0:T(8,128)(2,1)} fusion(bf16[4,144,7680]{2,1,0:T(8,128)(2,1)} %bitcast.61, pred[4,144]{1,0:T(4,128)(4,1)S(1)} %get-tuple-element.8, pred[4,144]{1,0:T(4,128)(4,1)S(1)} %get-tuple-element.7), kind=kLoop, calls=%fused_computation.3 | loop fusion | flops 8847360 | bytes 17695872 | tf_op jit(solution)/shard_map/jit(_where)/select_n | solution.py:92
  64.9 26.7 %all-to-all-done.2 = bf16[4,144,2560]{2,1,0:T(8,128)(2,1)} async-done(((bf16[4,144,2560]{2,1,0:T(8,128)(2,1)}), bf16[4,144,2560]{2,1,0:T(8,128)(2,1)}, u32[]{:S(2)}, u32[]{:S(2)}) %all-to-all-start.2) | async-done | bytes 2949152 | tf_op jit(solution)/shard_map/all_to_all | solution.py:101
  91.6 5.7 %all-to-all-start = ((bf16[4,144,7680]{2,1,0:T(8,128)(2,1)}), bf16[4,144,7680]{2,1,0:T(8,128)(2,1)}, u32[]{:S(2)}, u32[]{:S(2)}) async-start(bf16[4,144,7680]{2,1,0:T(8,128)(2,1)} %select_select_fusion), calls=%async_computation | async-start | bytes 17694720 | tf_op jit(solution)/shard_map/all_to_all | solution.py:100
  97.3 0.2 all-gather.6.cloned.1.call-start
  97.6 0.5 broadcast.237
  98.1 0.7 reduce.4
  99.1 2.7 fusion.43
  101.8 2.3 convolution_bitcast_fusion.1
  104.1 91.3 %all-to-all-done = bf16[4,144,7680]{2,1,0:T(8,128)(2,1)} async-done(((bf16[4,144,7680]{2,1,0:T(8,128)(2,1)}), bf16[4,144,7680]{2,1,0:T(8,128)(2,1)}, u32[]{:S(2)}, u32[]{:S(2)}) %all-to-all-start) | async-done | bytes 8847392 | tf_op jit(solution)/shard_map/all_to_all | solution.py:100
  195.4 4.0 %slice_bitcast_fusion.2 = (bf16[12,6,20,8,128]{4,3,2,1,0:T(8,128)(2,1)S(1)}, bf16[12,6,20,8,128]{4,3,2,1,0:T(8,128)(2,1)S(1)}, bf16[12,6,20,8,128]{4,3,2,1,0:T(8,128)(2,1)S(1)}) fusion(bf16[12,48,7680]{2,1,0:T(8,128)(2,1)} %bitcast.5), kind=kLoop, calls=%fused_computation.22 | loop fusion | bytes 17694720
  199.4 1.7 fusion
  201.2 2.0 convert_bitcast_fusion
  203.2 2.6 copy.30
  205.8 28.8 %all-gather.4.cloned.1.call-done = bf16[2560,2560]{1,0:T(8,128)(2,1)} async-done(((bf16[2560,640]{1,0:T(8,128)(2,1)}), bf16[2560,2560]{1,0:T(8,128)(2,1)}) %all-gather.4.cloned.1.call-update) | async-done | bytes 13107216 | tf_op jit(solution)/shard_map/all_gather | solution.py:43
  234.6 12.4 %multiply_convert_fusion = bf16[576,2560]{1,0:T(8,128)(2,1)S(1)} fusion(bf16[576,2560]{1,0:T(8,128)(2,1)} %bitcast.9, bf16[2560,2560]{1,0:T(8,128)(2,1)} %all-gather.4.cloned.1.call-done, bf16[72,8,20,128]{3,2,1,0:T(8,128)(2,1)} %bitcast.63, f32[576]{0:T(1024)S(1)} %reshape.360), kind=kOutput, calls=%fused_computation.4 | convolution fusion | flops 7555645440 | bytes 21956864 | tf_op jit(solution)/shard_map/dot_general | solution.py:41
  246.9 0.9 fusion.42
  247.8 0.5 convolution_bitcast_fusion
  248.3 0.2 copy-done.3
  248.5 0.7 pad_maximum_fusion
  249.2 44.1 %all-gather.6.cloned.1.call-done = f32[32,2560,8]{1,2,0:T(8,128)} async-done(((f32[2,2560,8]{1,2,0:T(8,128)}), f32[32,2560,8]{1,2,0:T(8,128)}) %all-gather.6.cloned.1.call-update) | async-done | bytes 2621456 | tf_op jit(solution)/shard_map/all_gather | solution.py:110
  293.3 2.5 reduce_sum.69
  (46 shorter events, 1.9 us)
Async XLA Ops:
  7.2 6.2 %copy-start = (bf16[240,2560]{1,0:T(8,128)(2,1)S(1)}, bf16[240,2560]{1,0:T(8,128)(2,1)}, u32[]{:S(2)}) copy-start(bf16[240,2560]{1,0:T(8,128)(2,1)} %param.8) | copy-start | bytes 3686404
  7.2 0.8 copy-start.5
  7.2 0.9 copy-start.6
  7.2 227.4 %all-gather.4.cloned.1.call-start = ((), (), s32[]{:S(2)}) async-start(), calls=%async_computation.4 | async-start | bytes 16384000 | tf_op jit(solution)/shard_map/all_gather | solution.py:43
  9.2 13.1 %all-to-all-start.1 = ((s32[4,1,3]{2,1,0:T(1,128)}), s32[4,1,3]{2,1,0:T(1,128)S(1)}, u32[]{:S(2)}, u32[]{:S(2)}) async-start(s32[4,1,3]{2,1,0:T(1,128)} %copy.27), calls=%async_computation.1 | async-start | bytes 4096 | tf_op jit(solution)/shard_map/all_to_all | solution.py:97
  13.4 4.2 %copy-start.2 = (s32[240]{0:T(256)S(1)}, s32[240]{0:T(256)}, u32[]{:S(2)}) copy-start(s32[240]{0:T(256)} %param.11) | copy-start | bytes 2884
  22.3 29.9 %all-to-all-start.3 = ((s32[4,1,144]{2,1,0:T(1,128)}), s32[4,1,144]{2,1,0:T(1,128)S(1)}, u32[]{:S(2)}, u32[]{:S(2)}) async-start(s32[4,1,144]{2,1,0:T(1,128)} %copy.31), calls=%async_computation.3 | async-start | bytes 8192 | tf_op jit(solution)/shard_map/all_to_all | solution.py:96
  52.1 39.5 %all-to-all-start.2 = ((bf16[4,144,2560]{2,1,0:T(8,128)(2,1)}), bf16[4,144,2560]{2,1,0:T(8,128)(2,1)}, u32[]{:S(2)}, u32[]{:S(2)}) async-start(bf16[4,144,2560]{2,1,0:T(8,128)(2,1)} %select_select_fusion.1), calls=%async_computation.2 | async-start | bytes 5898240 | tf_op jit(solution)/shard_map/all_to_all | solution.py:101
  64.9 34.2 %copy-start.4 = (bf16[2,2560,8]{1,2,0:T(8,128)(2,1)S(1)}, bf16[2,2560,8]{1,2,0:T(8,128)(2,1)}, u32[]{:S(2)}) copy-start(bf16[2,2560,8]{1,2,0:T(8,128)(2,1)} %param.10) | copy-start | bytes 245764
  91.6 103.8 %all-to-all-start = ((bf16[4,144,7680]{2,1,0:T(8,128)(2,1)}), bf16[4,144,7680]{2,1,0:T(8,128)(2,1)}, u32[]{:S(2)}, u32[]{:S(2)}) async-start(bf16[4,144,7680]{2,1,0:T(8,128)(2,1)} %select_select_fusion), calls=%async_computation | async-start | bytes 17694720 | tf_op jit(solution)/shard_map/all_to_all | solution.py:100
  97.3 196.0 %all-gather.6.cloned.1.call-start = ((), (), s32[]{:S(2)}) async-start(), calls=%async_computation.5 | async-start | bytes 2785280 | tf_op jit(solution)/shard_map/all_gather | solution.py:110
  246.9 1.6 copy-start.3
  247.8 48.0 %copy-start.1 = (bf16[240,2560]{1,0:T(8,128)(2,1)S(1)}, bf16[240,2560]{1,0:T(8,128)(2,1)}, u32[]{:S(2)}) copy-start(bf16[240,2560]{1,0:T(8,128)(2,1)} %param.8) | copy-start | bytes 3686404
Sparse Core Ops, SparseCore 0:
  9.6 224.9 all-gather.3
  249.4 43.9 all-gather.5
